TPU v7x, 32 devices: a whole 2x2x4 slice. The times are simulated.
32 devices in a mesh: groups: 2 (over y), shard: 4 (over z), pair: 4 (over x, core).
Axes of the slice: x: 2, y: 2, z: 4, core: 2. Of those that a mesh axis runs over, the one named last changes fastest.
Arguments:
- gradient: bfloat16 [2, 8, 512, 512], P('groups', None, 'shard'), parts along dimension 0, may hold values from -6.5 to 6.5, as said below
- momentum: bfloat16 [2, 8, 512, 512], P('groups', None, 'shard'), parts along dimension 0, may hold values from -6.5 to 6.5, as said below
Outputs:
- update: bfloat16 [2, 8, 512, 512], P('groups', None, 'shard'), parts along dimension 0
- new_momentum: bfloat16 [2, 8, 512, 512], P('groups', None, 'shard'), parts along dimension 0
There are 2 independent parts, one for each index of `groups`. A program takes and returns all parts, laid end to end along the dimension named above; each array names one. Nothing has to cross between parts.
Inputs may be any that keep to these rules, and one draw needn't show every extreme that they name: `gradient`: entries of order one. `momentum`: entries of order one.
All inputs are finite; a program needn't handle non-finite values.
Results may differ from a plain program's by a relative error of at most 0.0053.
Values may be sent and summed in bfloat16 or wider, within the bound.
A program may use at most 64 MiB of HBM per device.

v0:
```python
import jax
import jax.numpy as jnp
from jax import lax
from jax.sharding import PartitionSpec as P

damping = 0.1
decay_rate = 0.9


def from_partner(value, axis, apart):
    mask = 2**apart
    pairs = [(source, source ^ mask) for source in range(lax.axis_size(axis))]
    return lax.ppermute(value, axis, pairs)


def multiply(left_matrix, right_matrix):
    return jnp.dot(
        left_matrix,
        right_matrix,
        precision=lax.Precision.HIGHEST,
        preferred_element_type=jnp.float32,
    )


def gram_root(gram_matrix):
    block_size = gram_matrix.shape[0]
    identity = jnp.eye(block_size, dtype=jnp.float32)
    scaling = 2.0 * jnp.trace(gram_matrix) / block_size
    root_scale = jnp.sqrt(jnp.sqrt(scaling))
    scaled = gram_matrix / scaling
    leading = (5.0 * identity - scaled) / 4.0
    iterate = leading / root_scale
    squared = multiply(leading, leading)
    fourth = multiply(squared, squared)
    shifted = multiply(fourth, scaled)
    second = (5.0 * identity - shifted) / 4.0
    return multiply(iterate, second)


def local(gradient, momentum):
    new_momentum = (
        decay_rate * momentum.astype(jnp.float32) + gradient.astype(jnp.float32)
    ).astype(jnp.bfloat16)
    block_rows, block_cols, local_rows, block_size = gradient.shape
    half_cols = block_cols // 2
    half_width = block_size // 2
    shards = lax.axis_size("shard")
    position = lax.axis_index("pair")
    column_half = position // 2
    side_index = position % 2
    leading_side = side_index == 0
    grad_half = lax.dynamic_slice_in_dim(gradient, column_half * half_cols, half_cols, 1).reshape(
        shards, local_rows, block_size
    )
    mom_half = lax.dynamic_slice_in_dim(
        new_momentum, column_half * half_cols, half_cols, 1
    ).reshape(shards, local_rows, block_size)
    grad_recv, mom_recv = (
        lax.all_to_all(grad_half, "shard", split_axis=0, concat_axis=1, tiled=True),
        lax.all_to_all(mom_half, "shard", split_axis=0, concat_axis=1, tiled=True),
    )
    grad_block = grad_recv[0]
    mom_block = mom_recv[0]
    identity = jnp.eye(block_size, dtype=jnp.float32)
    oriented = jnp.where(leading_side, grad_block, grad_block.T)
    gram_matrix = (
        jnp.dot(oriented, oriented.T, preferred_element_type=jnp.float32) / block_size
        + damping * identity
    )
    own_root = gram_root(gram_matrix)
    partner = from_partner(own_root, "pair", 0)
    left_root = jnp.where(leading_side, own_root, partner)
    right_root = jnp.where(leading_side, partner, own_root)
    right_part = lax.dynamic_slice_in_dim(right_root, side_index * half_width, half_width, 1)
    partial_prod = multiply(mom_block.astype(jnp.float32), right_part)
    own_piece = multiply(left_root, partial_prod).astype(jnp.bfloat16)
    outgoing = own_piece.reshape(shards, local_rows, half_width)
    returned = lax.all_to_all(outgoing, "shard", split_axis=0, concat_axis=0, tiled=True)
    own_rows = returned.reshape(block_rows, half_cols, local_rows, half_width)
    gathered = lax.all_gather(own_rows[None], "pair", axis=0, tiled=True)
    update = (
        gathered.reshape(2, 2, block_rows, half_cols, local_rows, half_width)
        .transpose(2, 0, 3, 4, 1, 5)
        .reshape(block_rows, block_cols, local_rows, block_size)
    )
    return (update, new_momentum)


def solution(mesh):
    in_specs = (P("groups", None, "shard", None), P("groups", None, "shard", None))
    out_specs = (P("groups", None, "shard", None), P("groups", None, "shard", None))
    return jax.shard_map(local, mesh=mesh, in_specs=in_specs, out_specs=out_specs, check_vma=False)
```

profile of v0, /device:TPU:0, one launch (start us, length us, event | category | flops | bytes accessed | tf_op | source)
XLA Modules:
  0.0 102.2 jit_solution(1875327581618212463)
XLA Ops:
  7.2 1.9 %dynamic-slice_bitcast_fusion.1 = bf16[4,128,512]{2,1,0:T(8,128)(2,1)} fusion(bf16[1,8,128,512]{3,2,1,0:T(8,128)(2,1)} %param.2, s32[]{:T(128)S(6)} %select_n.44), kind=kLoop, calls=%fused_computation.23 | loop fusion | bytes 1048580 | tf_op jit(solution)/shard_map/reshape | solution.py:52
  9.1 6.3 %all-to-all-start = ((bf16[4,128,512]{2,1,0:T(8,128)(2,1)}), bf16[4,128,512]{2,1,0:T(8,128)(2,1)S(1)}, u32[]{:S(2)}, u32[]{:S(2)}) async-start(bf16[4,128,512]{2,1,0:T(8,128)(2,1)} %dynamic-slice_bitcast_fusion.1), calls=%async_computation | async-start | bytes 1048576 | tf_op jit(solution)/shard_map/all_to_all | solution.py:59
  15.4 14.5 %all-to-all-done = bf16[4,128,512]{2,1,0:T(8,128)(2,1)S(1)} async-done(((bf16[4,128,512]{2,1,0:T(8,128)(2,1)}), bf16[4,128,512]{2,1,0:T(8,128)(2,1)S(1)}, u32[]{:S(2)}, u32[]{:S(2)}) %all-to-all-start) | async-done | bytes 524320 | tf_op jit(solution)/shard_map/all_to_all | solution.py:59
  29.9 0.2 copy.12
  30.1 1.1 %select_reduce_fusion = (f32[]{:T(128)}, f32[512,512]{1,0:T(8,128)S(1)}) fusion(bf16[512,512]{1,0:T(8,128)(2,1)S(1)} %bitcast.22, bf16[512,512]{0,1:T(8,128)(2,1)S(1)} %copy.12, pred[]{:T(512)S(6)} %eq.17), kind=kOutput, calls=%fused_computation.11 | convolution fusion | flops 270270464 | bytes 2097157 | tf_op jit(solution)/shard_map/dot_general | solution.py:67
  31.9 2.0 %fusion.6 = f32[512,512]{1,0:T(8,128)S(1)} fusion(f32[512,512]{1,0:T(8,128)S(1)} %get-tuple-element.3, f32[]{:T(128)S(6)} %div.40), kind=kOutput, calls=%fused_computation.13 | convolution fusion | flops 1611923456 | bytes 2097156 | tf_op jit(solution)/shard_map/dot_general | solution.py:17
  33.9 1.8 %fusion.28 = f32[512,512]{1,0:T(8,128)S(1)} fusion(f32[512,512]{1,0:T(8,128)S(1)} %fusion.6), kind=kOutput, calls=%fused_computation.38 | convolution fusion | flops 1610612736 | bytes 2097152 | tf_op jit(solution)/shard_map/dot_general | solution.py:17
  35.7 1.9 %fusion.1 = f32[512,512]{1,0:T(8,128)S(1)} fusion(f32[512,512]{1,0:T(8,128)S(1)} %fusion.28, f32[512,512]{1,0:T(8,128)S(1)} %get-tuple-element.3, f32[]{:T(128)S(6)} %div.40), kind=kOutput, calls=%fused_computation.5 | convolution fusion | flops 1611923456 | bytes 3145732 | tf_op jit(solution)/shard_map/dot_general | solution.py:17
  37.6 0.0 copy-start
  37.6 0.0 copy-start.2
  37.7 2.0 %fusion.4 = f32[512,512]{1,0:T(8,128)S(1)} fusion(f32[512,512]{1,0:T(8,128)S(1)} %fusion.1, f32[]{:T(128)S(6)} %sqrt.7, f32[512,512]{1,0:T(8,128)S(1)} %get-tuple-element.3, f32[]{:T(128)S(6)} %div.40), kind=kOutput, calls=%fused_computation.9 | convolution fusion | flops 1612185600 | bytes 3145736 | tf_op jit(solution)/shard_map/dot_general | solution.py:17
  39.7 0.1 collective-permute-start
  39.7 0.0 copy-done
  39.7 0.0 copy-done.2
  39.8 0.4 add_convert_fusion
  40.1 0.0 copy-start.1
  40.1 0.9 dynamic-slice_bitcast_fusion
  41.0 0.2 copy-done.1
  41.3 4.1 %all-to-all-start.1 = ((bf16[4,128,512]{2,1,0:T(8,128)(2,1)}), bf16[4,128,512]{2,1,0:T(8,128)(2,1)}, u32[]{:S(2)}, u32[]{:S(2)}) async-start(bf16[4,128,512]{2,1,0:T(8,128)(2,1)} %dynamic-slice_bitcast_fusion), calls=%async_computation.1 | async-start | bytes 1048576 | tf_op jit(solution)/shard_map/all_to_all | solution.py:60
  45.4 0.0 all-gather.3.cloned.1.call-start
  45.5 15.4 %all-to-all-done.1 = bf16[4,128,512]{2,1,0:T(8,128)(2,1)} async-done(((bf16[4,128,512]{2,1,0:T(8,128)(2,1)}), bf16[4,128,512]{2,1,0:T(8,128)(2,1)}, u32[]{:S(2)}, u32[]{:S(2)}) %all-to-all-start.1) | async-done | bytes 524320 | tf_op jit(solution)/shard_map/all_to_all | solution.py:60
  60.9 0.0 collective-permute-done
  60.9 1.7 %fusion.9 = f32[512,256]{1,0:T(8,128)S(1)} fusion(bf16[512,512]{1,0:T(8,128)(2,1)} %bitcast.4, f32[512,512]{1,0:T(8,128)S(1)} %fusion.4, s32[]{:T(128)S(6)} %select_n.49, f32[512,512]{1,0:T(8,128)S(1)} %collective-permute-done, pred[]{:T(512)S(6)} %eq.17), kind=kOutput, calls=%fused_computation.15 | convolution fusion | flops 805437440 | bytes 2097157 | tf_op jit(solution)/shard_map/dot_general | solution.py:17
  62.6 1.0 convolution_convert_fusion
  63.6 12.0 %all_to_all.23 = bf16[4,128,256]{2,1,0:T(8,128)(2,1)} all-to-all(bf16[4,128,256]{2,1,0:T(8,128)(2,1)S(1)} %bitcast.23), channel_id=1, replica_groups=mesh['groups'=2,'shard'=4,'pair'=4] {'shard'}, dimensions={0} | all-to-all | bytes 524288 | tf_op jit(solution)/shard_map/all_to_all | solution.py:78
  75.6 0.0 all-gather.3.cloned.1.call-update
  75.6 16.0 %all-gather.3.cloned.1.call-done = bf16[16,128,256]{2,1,0:T(8,128)(2,1)} async-done(((bf16[4,128,256]{2,1,0:T(8,128)(2,1)}), bf16[16,128,256]{2,1,0:T(8,128)(2,1)}) %all-gather.3.cloned.1.call-update) | async-done | bytes 1048592 | tf_op jit(solution)/shard_map/all_gather | solution.py:80
  91.6 2.3 %copy.11 = bf16[1,2,4,128,2,256]{5,4,3,2,1,0:T(2,128)(2,1)S(1)} copy(bf16[1,2,4,128,2,256]{5,3,2,4,1,0:T(8,128)(2,1)} %bitcast.24) | data formatting | bytes 2097152 | tf_op jit(solution)/shard_map/transpose | solution.py:83
  93.9 1.5 %reshape.31 = bf16[1,8,128,512]{3,2,1,0:T(8,128)(2,1)} reshape(bf16[1,2,4,128,2,256]{5,4,3,2,1,0:T(2,128)(2,1)S(1)} %copy.11) | data formatting | bytes 2097152 | tf_op jit(solution)/shard_map/reshape | solution.py:84
Async XLA Ops:
  9.1 20.8 %all-to-all-start = ((bf16[4,128,512]{2,1,0:T(8,128)(2,1)}), bf16[4,128,512]{2,1,0:T(8,128)(2,1)S(1)}, u32[]{:S(2)}, u32[]{:S(2)}) async-start(bf16[4,128,512]{2,1,0:T(8,128)(2,1)} %dynamic-slice_bitcast_fusion.1), calls=%async_computation | async-start | bytes 1048576 | tf_op jit(solution)/shard_map/all_to_all | solution.py:59
  37.6 2.1 %copy-start = (bf16[1,8,128,512]{3,2,1,0:T(8,128)(2,1)S(1)}, bf16[1,8,128,512]{3,2,1,0:T(8,128)(2,1)}, u32[]{:S(2)}) copy-start(bf16[1,8,128,512]{3,2,1,0:T(8,128)(2,1)} %param.2) | copy-start | bytes 3145732
  37.6 2.1 %copy-start.2 = (bf16[1,8,128,512]{3,2,1,0:T(8,128)(2,1)S(1)}, bf16[1,8,128,512]{3,2,1,0:T(8,128)(2,1)}, u32[]{:S(2)}) copy-start(bf16[1,8,128,512]{3,2,1,0:T(8,128)(2,1)} %param.3) | copy-start | bytes 3145732
  39.7 21.2 %collective-permute-start = (f32[512,512]{1,0:T(8,128)S(1)}, f32[512,512]{1,0:T(8,128)S(1)}, u32[]{:S(2)}, u32[]{:S(2)}) collective-permute-start(f32[512,512]{1,0:T(8,128)S(1)} %fusion.4), channel_id=1, source_target_pairs={{0,1},{1,0},{2,3},{3,2},{4,5},{5,4},{6,7},{7,6},{8,9},{9,8},{10,11... | collective-permute-start | bytes 3145736 | tf_op jit(solution)/shard_map/ppermute | solution.py:13
  40.1 1.1 %copy-start.1 = (bf16[1,8,128,512]{3,2,1,0:T(8,128)(2,1)}, bf16[1,8,128,512]{3,2,1,0:T(8,128)(2,1)S(1)}, u32[]{:S(2)}) copy-start(bf16[1,8,128,512]{3,2,1,0:T(8,128)(2,1)S(1)} %add_convert_fusion) | copy-start | bytes 3145732
  41.3 19.6 %all-to-all-start.1 = ((bf16[4,128,512]{2,1,0:T(8,128)(2,1)}), bf16[4,128,512]{2,1,0:T(8,128)(2,1)}, u32[]{:S(2)}, u32[]{:S(2)}) async-start(bf16[4,128,512]{2,1,0:T(8,128)(2,1)} %dynamic-slice_bitcast_fusion), calls=%async_computation.1 | async-start | bytes 1048576 | tf_op jit(solution)/shard_map/all_to_all | solution.py:60
  45.4 46.2 %all-gather.3.cloned.1.call-start = ((), (), s32[]{:S(2)}) async-start(), calls=%async_computation.3 | async-start | bytes 1310720 | tf_op jit(solution)/shard_map/all_gather | solution.py:80
Sparse Core Ops, SparseCore 0:
  75.7 15.7 all-gather.2
where the time goes:
time: 103 us; the launch traced here: 102 us
  waiting for transfers between devices  45.9 us (45%)
  between operations  14.9 us (14%)
  blocking collectives  12 us (12%)
  matrix products  11.5 us (11%)
  starting transfers between devices  10.6 us (10%)
  local copies, waits for them, and re-layouts  7.03 us (7%)
    all_gather x1, waiting for transfers between devices, local(): gathered = lax.all_gather(own_rows[None], 'pair', axis=0, tiled=True)  16 us
    all_to_all x1, waiting for transfers between devices, local(): lax.all_to_all(mom_half, 'shard', split_axis=0, concat_axis=1, tiled=True)  15.4 us
    all_to_all x1, waiting for transfers between devices, local(): lax.all_to_all(grad_half, 'shard', split_axis=0, concat_axis=1, tiled=True)  14.5 us
    all_to_all x1, blocking collectives, local(): lax.all_to_all(outgoing, 'shard', split_axis=0, concat_axis=0, tiled=True)  12 us
    dot_general x6, matrix products, multiply(): jnp.dot(left_matrix, right_matrix, precision=lax.Precision.HIGHEST, prefe...  10.4 us
    all_to_all x1, starting transfers between devices, local(): lax.all_to_all(grad_half, 'shard', split_axis=0, concat_axis=1, tiled=True)  6.35 us
    all_to_all x1, starting transfers between devices, local(): lax.all_to_all(mom_half, 'shard', split_axis=0, concat_axis=1, tiled=True)  4.14 us
    transpose x1, local copies, waits for them, and re-layouts, local(): update = gathered.reshape(2, 2, block_rows, half_cols, local_rows, half_w...  2.3 us
  transfers between devices with their start and end apart: 4, of which 3 were waited for; matrix products, arithmetic and copies ran while one was open for 1% of the time, Pallas kernels for 0%

commit v1 on v0

--- a/solution.py
+++ b/solution.py
@@ -1,10 +1,15 @@
+import functools
+
 import jax
 import jax.numpy as jnp
 from jax import lax
+from jax.experimental import pallas as pl
+from jax.experimental.pallas import tpu as pltpu
 from jax.sharding import PartitionSpec as P
 
 damping = 0.1
 decay_rate = 0.9
+MESH = pl.DeviceIdType.MESH
 
 
 def from_partner(value, axis, apart):
@@ -37,7 +42,7 @@
     return multiply(iterate, second)
 
 
-def local(gradient, momentum):
+def by_collectives(gradient, momentum):
     new_momentum = (
         decay_rate * momentum.astype(jnp.float32) + gradient.astype(jnp.float32)
     ).astype(jnp.bfloat16)
@@ -86,6 +91,296 @@
     return (update, new_momentum)
 
 
+def dot(left, right, contract=((1,), (0,))):
+    return lax.dot_general(
+        left, right, (contract, ((), ())), preferred_element_type=jnp.float32
+    )
+
+
+def diagonal(rows, cols, offset):
+    row = lax.broadcasted_iota(jnp.int32, (rows, cols), 0)
+    col = lax.broadcasted_iota(jnp.int32, (rows, cols), 1)
+    return row == col + offset
+
+
+def step_kernel(
+    shards,
+    half_cols,
+    grad,
+    mom,
+    update,
+    grad_block,
+    mom_block,
+    new_block,
+    left_scaled,
+    left_square,
+    right_scaled,
+    right_square,
+    right_full,
+    factor,
+    product,
+    outgoing,
+    local_sem,
+    z_send,
+    z_recv,
+    pass_send,
+    pass_recv,
+    back_send,
+    back_recv,
+    across_send,
+    across_recv,
+    twin_send,
+    twin_recv,
+):
+    rows, size = grad.shape[1:]
+    half = rows // 2
+    width = size // 2
+    shard = lax.axis_index("shard")
+    pair = lax.axis_index("pair")
+    side = lax.rem(pair, 2)
+    column = pair // 2
+    twin = pair + 1 - 2 * side
+    across = lax.rem(pair + 2, 4)
+
+    def block_of(column_half, owner):
+        return (owner // half_cols) * 2 * half_cols + column_half * half_cols + lax.rem(
+            owner, half_cols
+        )
+
+    def other(step):
+        return lax.rem(shard + step, shards)
+
+    barrier = pltpu.get_barrier_semaphore()
+    for step in range(1, shards):
+        pl.semaphore_signal(
+            barrier, inc=1, device_id={"shard": other(step)}, device_id_type=MESH
+        )
+    for peer in (twin, across):
+        pl.semaphore_signal(barrier, inc=1, device_id={"pair": peer}, device_id_type=MESH)
+    pl.semaphore_wait(barrier, shards + 1)
+
+    def piece(owner):
+        return pl.ds(pl.multiple_of(owner * rows + side * half, half), half)
+
+    def whole_piece(owner):
+        return pl.ds(pl.multiple_of(owner * rows, rows), rows)
+
+    own_half = pl.ds(pl.multiple_of(side * half, half), half)
+    sends = []
+    locals_ = []
+    for kind, (source, block) in enumerate(((grad, grad_block), (mom, mom_block))):
+        kind_sends = []
+        for step in range(1, shards):
+            target = other(step)
+            copy = pltpu.make_async_remote_copy(
+                src_ref=source.at[block_of(column, target), own_half],
+                dst_ref=block.at[piece(shard)],
+                send_sem=z_send.at[kind, step - 1],
+                recv_sem=z_recv.at[kind, step - 1],
+                device_id={"shard": target},
+                device_id_type=MESH,
+            )
+            copy.start()
+            kind_sends.append(copy)
+        sends.append(kind_sends)
+        copy = pltpu.make_async_copy(
+            source.at[block_of(column, shard)],
+            block.at[whole_piece(shard)],
+            local_sem.at[kind],
+        )
+        copy.start()
+        locals_.append(copy)
+
+    def collect(kind, block):
+        passes = []
+        for step in range(1, shards):
+            sends[kind][step - 1].wait_recv()
+            origin = lax.rem(shard + shards - step, shards)
+            copy = pltpu.make_async_remote_copy(
+                src_ref=block.at[piece(origin)],
+                dst_ref=block.at[piece(origin)],
+                send_sem=pass_send.at[kind, step - 1],
+                recv_sem=pass_recv.at[kind, step - 1],
+                device_id={"pair": twin},
+                device_id_type=MESH,
+            )
+            copy.start()
+            passes.append(copy)
+        for copy in passes:
+            copy.wait_recv()
+        locals_[kind].wait()
+        return passes
+
+    grad_passes = collect(0, grad_block)
+
+    values = grad_block[...]
+    wide = values.astype(jnp.float32)
+    total = jnp.sum(wide * wide, keepdims=True)
+    scaling = 2.0 * (total / size + damping * size) / size
+    inverse = 1.0 / scaling
+    identity = diagonal(size, size, 0)
+
+    def prepare(gram, scaled_ref, square_ref, full_ref):
+        scaled = gram * (inverse / size) + jnp.where(identity, damping * inverse, 0.0)
+        if full_ref is not None:
+            full_ref[...] = scaled
+        narrow = scaled.astype(jnp.bfloat16)
+        scaled_ref[...] = narrow
+        square_ref[...] = (
+            jnp.where(identity, 0.5625, 0.0) - 0.625 * scaled + dot(narrow, narrow) / 16.0
+        ).astype(jnp.bfloat16)
+
+    prepare(dot(values, values, ((0,), (0,))), right_scaled, right_square, right_full)
+    prepare(dot(values, values, ((1,), (1,))), left_scaled, left_square, None)
+
+    def newton(first, scaled_ref, square_ref):
+        second = first + dot(square_ref[...], first.astype(jnp.bfloat16))
+        third = second + dot(square_ref[...], second.astype(jnp.bfloat16))
+        return (first + third) * -0.3125 + dot(
+            scaled_ref[...], third.astype(jnp.bfloat16)
+        ) / 16.0
+
+    own_cols = pl.ds(pl.multiple_of(side * width, width), width)
+    first = right_full[:, own_cols]
+    factor[...] = (
+        newton(first, right_scaled, right_square)
+        + jnp.where(diagonal(size, width, side * width), 0.5625, 0.0)
+    ).astype(jnp.bfloat16)
+
+    mom_passes = collect(1, mom_block)
+    new_block[...] = (
+        decay_rate * mom_block[...].astype(jnp.float32) + grad_block[...].astype(jnp.float32)
+    ).astype(jnp.bfloat16)
+    product[...] = new_block[:, own_cols].astype(jnp.float32) + dot(
+        new_block[...], factor[...]
+    )
+    first = dot(left_scaled[...], product[...].astype(jnp.bfloat16))
+    outgoing[...] = (
+        (newton(first, left_scaled, left_square) + 1.5625 * product[...])
+        / jnp.sqrt(scaling)
+    ).astype(jnp.bfloat16)
+
+    backs = []
+    for step in range(1, shards):
+        target = other(step)
+        copy = pltpu.make_async_remote_copy(
+            src_ref=outgoing.at[whole_piece(target)],
+            dst_ref=update.at[block_of(column, shard), :, own_cols],
+            send_sem=back_send.at[step - 1],
+            recv_sem=back_recv.at[step - 1],
+            device_id={"shard": target},
+            device_id_type=MESH,
+        )
+        copy.start()
+        backs.append(copy)
+    own_copy = pltpu.make_async_copy(
+        outgoing.at[whole_piece(shard)],
+        update.at[block_of(column, shard), :, own_cols],
+        local_sem.at[0],
+    )
+    own_copy.start()
+
+    def hand_on(source, slot, owner_column, origin, send, recv, index, peer):
+        copy = pltpu.make_async_remote_copy(
+            src_ref=source,
+            dst_ref=update.at[block_of(owner_column, origin), :, own_cols],
+            send_sem=send.at[index],
+            recv_sem=recv.at[index],
+            device_id={"pair": peer},
+            device_id_type=MESH,
+        )
+        copy.start()
+        return copy
+
+    acrosses = []
+    twins = []
+    for step in range(shards):
+        origin = lax.rem(shard + shards - step, shards)
+        if step:
+            backs[step - 1].wait_recv()
+            source = update.at[block_of(column, origin), :, own_cols]
+        else:
+            source = outgoing.at[whole_piece(shard)]
+        acrosses.append(
+            hand_on(source, None, column, origin, across_send, across_recv, step, across)
+        )
+        twins.append(hand_on(source, None, column, origin, twin_send, twin_recv, step, twin))
+    for step in range(shards):
+        origin = lax.rem(shard + shards - step, shards)
+        acrosses[step].wait_recv()
+        source = update.at[block_of(1 - column, origin), :, own_cols]
+        twins.append(
+            hand_on(
+                source, None, 1 - column, origin, twin_send, twin_recv, shards + step, twin
+            )
+        )
+    for copy in twins:
+        copy.wait_recv()
+    own_copy.wait()
+    for copy in (
+        sends[0] + sends[1] + grad_passes + mom_passes + backs + acrosses + twins
+    ):
+        copy.wait_send()
+
+
+def by_kernel(gradient, momentum):
+    new_momentum = (
+        decay_rate * momentum.astype(jnp.float32) + gradient.astype(jnp.float32)
+    ).astype(jnp.bfloat16)
+    block_rows, block_cols, rows, size = gradient.shape
+    shards = lax.axis_size("shard")
+    count = block_rows * block_cols
+    flat = (count, rows, size)
+    width = size // 2
+    vmem = pltpu.VMEM
+    dma = pltpu.SemaphoreType.DMA
+    update = pl.pallas_call(
+        functools.partial(step_kernel, shards, block_cols // 2),
+        out_shape=jax.ShapeDtypeStruct(flat, jnp.bfloat16),
+        in_specs=[pl.BlockSpec(memory_space=pl.ANY)] * 2,
+        out_specs=pl.BlockSpec(memory_space=pl.ANY),
+        scratch_shapes=[
+            vmem((size, size), jnp.bfloat16),
+            vmem((size, size), jnp.bfloat16),
+            vmem((size, size), jnp.bfloat16),
+            vmem((size, size), jnp.bfloat16),
+            vmem((size, size), jnp.bfloat16),
+            vmem((size, size), jnp.bfloat16),
+            vmem((size, size), jnp.bfloat16),
+            vmem((size, size), jnp.float32),
+            vmem((size, width), jnp.bfloat16),
+            vmem((size, width), jnp.float32),
+            vmem((size, width), jnp.bfloat16),
+            dma((2,)),
+            dma((2, shards - 1)),
+            dma((2, shards - 1)),
+            dma((2, shards - 1)),
+            dma((2, shards - 1)),
+            dma((shards - 1,)),
+            dma((shards - 1,)),
+            dma((shards,)),
+            dma((shards,)),
+            dma((2 * shards,)),
+            dma((2 * shards,)),
+        ],
+        compiler_params=pltpu.CompilerParams(collective_id=0, has_side_effects=True),
+    )(gradient.reshape(flat), momentum.reshape(flat))
+    return (update.reshape(gradient.shape), new_momentum)
+
+
+def local(gradient, momentum):
+    block_rows, block_cols, rows, size = gradient.shape
+    shards = lax.axis_size("shard")
+    fits = (
+        lax.axis_size("pair") == 4
+        and block_rows * block_cols == 2 * shards
+        and rows * shards == size
+        and rows % 32 == 0
+        and size % 256 == 0
+    )
+    return (by_kernel if fits else by_collectives)(gradient, momentum)
+
+
 def solution(mesh):
     in_specs = (P("groups", None, "shard", None), P("groups", None, "shard", None))
     out_specs = (P("groups", None, "shard", None), P("groups", None, "shard", None))

time: 103 us -> 38 us (0.37)
  waiting for transfers between devices: 45.9 us -> 0 us
  Pallas kernels: 0 us -> 34.9 us
  between operations: 14.9 us -> 0.68 us
  blocking collectives: 12 us -> 0 us
  matrix products: 11.5 us -> 0 us
  starting transfers between devices: 10.6 us -> 0 us
  local copies, waits for them, and re-layouts: 7.03 us -> 0.98 us
    pallas_call x0 -> x1, Pallas kernels: none -> 34.9 us  [by_kernel(): pl.pallas_call(functools.partial(step_kernel, shards, block_cols // 2), o...]
    all_to_all x2 -> x0, waiting for transfers between devices: 29.9 us -> none  [the longest x1 15.4 us: local(): lax.all_to_all(mom_half, 'shard', split_axis=0, concat_axis=1, tiled=True)]
    all_gather x1 -> x0, waiting for transfers between devices: 16 us -> none  [local(): gathered = lax.all_gather(own_rows[None], 'pair', axis=0, tiled=True)]
    all_to_all x1 -> x0, blocking collectives: 12 us -> none  [local(): lax.all_to_all(outgoing, 'shard', split_axis=0, concat_axis=0, tiled=True)]
    dot_general x7 -> x0, matrix products: 11.5 us -> none  [the longest x6 10.4 us: multiply(): jnp.dot(left_matrix, right_matrix, precision=lax.Precision.HIGHEST, prefe...]
    all_to_all x2 -> x0, starting transfers between devices: 10.5 us -> none  [the longest x1 6.35 us: local(): lax.all_to_all(grad_half, 'shard', split_axis=0, concat_axis=1, tiled=True)]
    reshape x3 -> x0, local copies, waits for them, and re-layouts: 4.25 us -> none  [the longest x1 1.87 us: local(): lax.dynamic_slice_in_dim(gradient, column_half * half_cols, half_cols, 1)]
    transpose x1 -> x0, local copies, waits for them, and re-layouts: 2.3 us -> none  [local(): update = gathered.reshape(2, 2, block_rows, half_cols, local_rows, half_w...]
  transfers between devices with their start and end apart: 4 -> 0, of which waited for: 3 -> 0; matrix products, arithmetic and copies ran while one was open for 1% -> 0% of each run, Pallas kernels for 0% -> 0%
where the time goes in v1:
time: 38 us; the launch traced here: 37.9 us
  Pallas kernels  34.9 us (92%)
  other arithmetic  1.3 us (3%)
  local copies, waits for them, and re-layouts  0.98 us (3%)
  between operations  0.68 us (2%)
    pallas_call x1, Pallas kernels, by_kernel(): pl.pallas_call(functools.partial(step_kernel, shards, block_cols // 2), o...  34.9 us
    convert_element_type x1, other arithmetic, by_kernel(): new_momentum = (decay_rate * momentum.astype(jnp.float32) + gradient.asty...  1.3 us
    unnamed x7, local copies, waits for them, and re-layouts  0.98 us

profile of v1, /device:TPU:0, one launch (start us, length us, event | category | flops | bytes accessed | tf_op | source)
XLA Modules:
  0.0 37.9 jit_solution(13797666137919805958)
XLA Ops:
  0.6 0.0 copy-start
  0.6 0.0 copy-start.1
  0.6 34.9 %shard_map.41 = bf16[8,128,512]{2,1,0:T(8,128)(2,1)} custom-call(bf16[8,128,512]{2,1,0:T(8,128)(2,1)} %bitcast.3, bf16[8,128,512]{2,1,0:T(8,128)(2,1)} %bitcast.4), custom_call_target="tpu_custom_call" | custom-call | tf_op jit(solution)/shard_map/pallas_call | solution.py:337
  35.6 0.0 copy-done
  35.6 0.0 copy-done.1
  35.6 0.0 copy-start.2
  35.6 1.3 %add_convert_fusion = bf16[1,8,128,512]{3,2,1,0:T(8,128)(2,1)} fusion(bf16[1,8,128,512]{3,2,1,0:T(8,128)(2,1)S(1)} %copy-done, bf16[1,8,128,512]{3,2,1,0:T(8,128)(2,1)S(1)} %copy-done.1), kind=kLoop, calls=%fused_computation | loop fusion | flops 2621440 | bytes 3145728 | tf_op jit(solution)/shard_map/convert_element_type | solution.py:329
  36.9 0.0 copy-done.2
  36.9 1.0 %copy.5 = bf16[1,8,128,512]{3,2,1,0:T(8,128)(2,1)} copy(bf16[1,8,128,512]{3,2,1,0:T(8,128)(2,1)S(1)} %bitcast.5) | data formatting | bytes 2097152
Async XLA Ops:
  0.6 34.9 %copy-start = (bf16[1,8,128,512]{3,2,1,0:T(8,128)(2,1)S(1)}, bf16[1,8,128,512]{3,2,1,0:T(8,128)(2,1)}, u32[]{:S(2)}) copy-start(bf16[1,8,128,512]{3,2,1,0:T(8,128)(2,1)} %param.2) | copy-start | bytes 3145732
  0.6 34.9 %copy-start.1 = (bf16[1,8,128,512]{3,2,1,0:T(8,128)(2,1)S(1)}, bf16[1,8,128,512]{3,2,1,0:T(8,128)(2,1)}, u32[]{:S(2)}) copy-start(bf16[1,8,128,512]{3,2,1,0:T(8,128)(2,1)} %param.3) | copy-start | bytes 3145732
  35.6 1.3 %copy-start.2 = (bf16[8,128,512]{2,1,0:T(8,128)(2,1)S(1)}, bf16[8,128,512]{2,1,0:T(8,128)(2,1)}, u32[]{:S(2)}) copy-start(bf16[8,128,512]{2,1,0:T(8,128)(2,1)} %shard_map.41) | copy-start | bytes 3145732

commit v2 on v1

--- a/solution.py
+++ b/solution.py
@@ -109,15 +109,18 @@
     grad,
     mom,
     update,
+    new_mom,
+    grad_rows,
+    mom_rows,
     grad_block,
     mom_block,
-    new_block,
+    full,
     left_scaled,
     left_square,
     right_scaled,
     right_square,
-    right_full,
-    factor,
+    left_factor,
+    right_factor,
     product,
     outgoing,
     local_sem,
@@ -132,7 +135,7 @@
     twin_send,
     twin_recv,
 ):
-    rows, size = grad.shape[1:]
+    count, rows, size = grad.shape
     half = rows // 2
     width = size // 2
     shard = lax.axis_index("shard")
@@ -141,22 +144,32 @@
     column = pair // 2
     twin = pair + 1 - 2 * side
     across = lax.rem(pair + 2, 4)
+    order = peer_order(shards)
+    peers = []
+    for mask in order:
+        peer = shard
+        bit = 1
+        while bit < shards:
+            if mask & bit:
+                peer = peer + bit - 2 * bit * lax.rem(shard // bit, 2)
+            bit *= 2
+        peers.append(peer)
 
     def block_of(column_half, owner):
         return (owner // half_cols) * 2 * half_cols + column_half * half_cols + lax.rem(
             owner, half_cols
         )
 
-    def other(step):
-        return lax.rem(shard + step, shards)
-
     barrier = pltpu.get_barrier_semaphore()
-    for step in range(1, shards):
-        pl.semaphore_signal(
-            barrier, inc=1, device_id={"shard": other(step)}, device_id_type=MESH
-        )
+    for peer in peers:
+        pl.semaphore_signal(barrier, inc=1, device_id={"shard": peer}, device_id_type=MESH)
     for peer in (twin, across):
         pl.semaphore_signal(barrier, inc=1, device_id={"pair": peer}, device_id_type=MESH)
+    loads = []
+    for kind, (source, local_rows) in enumerate(((grad, grad_rows), (mom, mom_rows))):
+        copy = pltpu.make_async_copy(source, local_rows, local_sem.at[kind])
+        copy.start()
+        loads.append(copy)
     pl.semaphore_wait(barrier, shards + 1)
 
     def piece(owner):
@@ -166,52 +179,53 @@
         return pl.ds(pl.multiple_of(owner * rows, rows), rows)
 
     own_half = pl.ds(pl.multiple_of(side * half, half), half)
+    own_cols = pl.ds(pl.multiple_of(side * width, width), width)
     sends = []
-    locals_ = []
     for kind, (source, block) in enumerate(((grad, grad_block), (mom, mom_block))):
         kind_sends = []
-        for step in range(1, shards):
-            target = other(step)
+        for index, target in enumerate(peers):
             copy = pltpu.make_async_remote_copy(
                 src_ref=source.at[block_of(column, target), own_half],
                 dst_ref=block.at[piece(shard)],
-                send_sem=z_send.at[kind, step - 1],
-                recv_sem=z_recv.at[kind, step - 1],
+                send_sem=z_send.at[kind, index],
+                recv_sem=z_recv.at[kind, index],
                 device_id={"shard": target},
                 device_id_type=MESH,
             )
             copy.start()
             kind_sends.append(copy)
         sends.append(kind_sends)
-        copy = pltpu.make_async_copy(
-            source.at[block_of(column, shard)],
-            block.at[whole_piece(shard)],
-            local_sem.at[kind],
-        )
-        copy.start()
-        locals_.append(copy)
+
+    def combine(momentum, gradient):
+        return (
+            decay_rate * momentum.astype(jnp.float32) + gradient.astype(jnp.float32)
+        ).astype(jnp.bfloat16)
+
+    for copy in loads:
+        copy.wait()
+    for index in range(count):
+        new_mom[index] = combine(mom_rows[index], grad_rows[index])
+    grad_block[whole_piece(shard), :] = grad_rows[block_of(column, shard)]
 
     def collect(kind, block):
         passes = []
-        for step in range(1, shards):
-            sends[kind][step - 1].wait_recv()
-            origin = lax.rem(shard + shards - step, shards)
+        for index, origin in enumerate(peers):
+            sends[kind][index].wait_recv()
             copy = pltpu.make_async_remote_copy(
                 src_ref=block.at[piece(origin)],
                 dst_ref=block.at[piece(origin)],
-                send_sem=pass_send.at[kind, step - 1],
-                recv_sem=pass_recv.at[kind, step - 1],
+                send_sem=pass_send.at[kind, index],
+                recv_sem=pass_recv.at[kind, index],
                 device_id={"pair": twin},
                 device_id_type=MESH,
             )
             copy.start()
             passes.append(copy)
-        for copy in passes:
-            copy.wait_recv()
-        locals_[kind].wait()
         return passes
 
     grad_passes = collect(0, grad_block)
+    for copy in grad_passes:
+        copy.wait_recv()
 
     values = grad_block[...]
     wide = values.astype(jnp.float32)
@@ -220,18 +234,14 @@
     inverse = 1.0 / scaling
     identity = diagonal(size, size, 0)
 
-    def prepare(gram, scaled_ref, square_ref, full_ref):
+    def prepare(gram, scaled_ref, square_ref):
         scaled = gram * (inverse / size) + jnp.where(identity, damping * inverse, 0.0)
-        if full_ref is not None:
-            full_ref[...] = scaled
+        full[...] = scaled
         narrow = scaled.astype(jnp.bfloat16)
         scaled_ref[...] = narrow
         square_ref[...] = (
             jnp.where(identity, 0.5625, 0.0) - 0.625 * scaled + dot(narrow, narrow) / 16.0
         ).astype(jnp.bfloat16)
-
-    prepare(dot(values, values, ((0,), (0,))), right_scaled, right_square, right_full)
-    prepare(dot(values, values, ((1,), (1,))), left_scaled, left_square, None)
 
     def newton(first, scaled_ref, square_ref):
         second = first + dot(square_ref[...], first.astype(jnp.bfloat16))
@@ -240,50 +250,63 @@
             scaled_ref[...], third.astype(jnp.bfloat16)
         ) / 16.0
 
-    own_cols = pl.ds(pl.multiple_of(side * width, width), width)
-    first = right_full[:, own_cols]
-    factor[...] = (
-        newton(first, right_scaled, right_square)
+    prepare(dot(values, values, ((0,), (0,))), right_scaled, right_square)
+    right_factor[...] = (
+        newton(full[:, own_cols], right_scaled, right_square)
         + jnp.where(diagonal(size, width, side * width), 0.5625, 0.0)
     ).astype(jnp.bfloat16)
-
+    prepare(dot(values, values, ((1,), (1,))), left_scaled, left_square)
+    left_factor[...] = (
+        newton(full[...], left_scaled, left_square) + jnp.where(identity, 0.5625, 0.0)
+    ).astype(jnp.bfloat16)
+
+    def multiply_rows(new_rows, own_part, owner):
+        product[whole_piece(owner), :] = own_part.astype(jnp.float32) + dot(
+            new_rows, right_factor[...]
+        )
+
+    own_block = block_of(column, shard)
+    multiply_rows(new_mom[own_block], new_mom[own_block, :, own_cols], shard)
     mom_passes = collect(1, mom_block)
-    new_block[...] = (
-        decay_rate * mom_block[...].astype(jnp.float32) + grad_block[...].astype(jnp.float32)
-    ).astype(jnp.bfloat16)
-    product[...] = new_block[:, own_cols].astype(jnp.float32) + dot(
-        new_block[...], factor[...]
-    )
-    first = dot(left_scaled[...], product[...].astype(jnp.bfloat16))
-    outgoing[...] = (
-        (newton(first, left_scaled, left_square) + 1.5625 * product[...])
-        / jnp.sqrt(scaling)
-    ).astype(jnp.bfloat16)
+    for copy, origin in zip(mom_passes, peers):
+        copy.wait_recv()
+        new_rows = combine(mom_block[whole_piece(origin), :], grad_block[whole_piece(origin), :])
+        own_part = combine(
+            mom_block[whole_piece(origin), own_cols], grad_block[whole_piece(origin), own_cols]
+        )
+        multiply_rows(new_rows, own_part, origin)
+
+    outer = 1.0 / jnp.sqrt(scaling)
+    narrow_product = product[...].astype(jnp.bfloat16)
+
+    def update_rows(owner):
+        return (
+            (
+                product[whole_piece(owner), :]
+                + dot(left_factor[whole_piece(owner), :], narrow_product)
+            )
+            * outer
+        ).astype(jnp.bfloat16)
 
     backs = []
-    for step in range(1, shards):
-        target = other(step)
+    for index, target in enumerate(peers):
+        outgoing[index] = update_rows(target)
         copy = pltpu.make_async_remote_copy(
-            src_ref=outgoing.at[whole_piece(target)],
-            dst_ref=update.at[block_of(column, shard), :, own_cols],
-            send_sem=back_send.at[step - 1],
-            recv_sem=back_recv.at[step - 1],
+            src_ref=outgoing.at[index],
+            dst_ref=update.at[own_block, :, own_cols],
+            send_sem=back_send.at[index],
+            recv_sem=back_recv.at[index],
             device_id={"shard": target},
             device_id_type=MESH,
         )
         copy.start()
         backs.append(copy)
-    own_copy = pltpu.make_async_copy(
-        outgoing.at[whole_piece(shard)],
-        update.at[block_of(column, shard), :, own_cols],
-        local_sem.at[0],
-    )
-    own_copy.start()
-
-    def hand_on(source, slot, owner_column, origin, send, recv, index, peer):
+    update[own_block, :, own_cols] = update_rows(shard)
+
+    def hand_on(block, send, recv, index, peer):
         copy = pltpu.make_async_remote_copy(
-            src_ref=source,
-            dst_ref=update.at[block_of(owner_column, origin), :, own_cols],
+            src_ref=update.at[block, :, own_cols],
+            dst_ref=update.at[block, :, own_cols],
             send_sem=send.at[index],
             recv_sem=recv.at[index],
             device_id={"pair": peer},
@@ -294,39 +317,37 @@
 
     acrosses = []
     twins = []
-    for step in range(shards):
-        origin = lax.rem(shard + shards - step, shards)
-        if step:
-            backs[step - 1].wait_recv()
-            source = update.at[block_of(column, origin), :, own_cols]
-        else:
-            source = outgoing.at[whole_piece(shard)]
-        acrosses.append(
-            hand_on(source, None, column, origin, across_send, across_recv, step, across)
-        )
-        twins.append(hand_on(source, None, column, origin, twin_send, twin_recv, step, twin))
-    for step in range(shards):
-        origin = lax.rem(shard + shards - step, shards)
-        acrosses[step].wait_recv()
-        source = update.at[block_of(1 - column, origin), :, own_cols]
+
+    def take_across(index, origin):
+        acrosses[index].wait_recv()
         twins.append(
-            hand_on(
-                source, None, 1 - column, origin, twin_send, twin_recv, shards + step, twin
-            )
-        )
+            hand_on(block_of(1 - column, origin), twin_send, twin_recv, shards + index, twin)
+        )
+
+    origins = [shard] + peers
+    for index, origin in enumerate(origins):
+        if index:
+            backs[index - 1].wait_recv()
+        block = block_of(column, origin)
+        acrosses.append(hand_on(block, across_send, across_recv, index, across))
+        twins.append(hand_on(block, twin_send, twin_recv, index, twin))
+        if index:
+            take_across(index - 1, origins[index - 1])
+    take_across(shards - 1, origins[-1])
     for copy in twins:
         copy.wait_recv()
-    own_copy.wait()
     for copy in (
         sends[0] + sends[1] + grad_passes + mom_passes + backs + acrosses + twins
     ):
         copy.wait_send()
 
 
+def peer_order(shards):
+    masks = list(range(1, shards))
+    return masks[:1] + masks[:0:-1]
+
+
 def by_kernel(gradient, momentum):
-    new_momentum = (
-        decay_rate * momentum.astype(jnp.float32) + gradient.astype(jnp.float32)
-    ).astype(jnp.bfloat16)
     block_rows, block_cols, rows, size = gradient.shape
     shards = lax.axis_size("shard")
     count = block_rows * block_cols
@@ -334,23 +355,26 @@
     width = size // 2
     vmem = pltpu.VMEM
     dma = pltpu.SemaphoreType.DMA
-    update = pl.pallas_call(
+    square = vmem((size, size), jnp.bfloat16)
+    update, new_momentum = pl.pallas_call(
         functools.partial(step_kernel, shards, block_cols // 2),
-        out_shape=jax.ShapeDtypeStruct(flat, jnp.bfloat16),
+        out_shape=[pltpu.VMEM(flat, jnp.bfloat16)] * 2,
         in_specs=[pl.BlockSpec(memory_space=pl.ANY)] * 2,
-        out_specs=pl.BlockSpec(memory_space=pl.ANY),
+        out_specs=[pl.BlockSpec(memory_space=pltpu.VMEM)] * 2,
         scratch_shapes=[
-            vmem((size, size), jnp.bfloat16),
-            vmem((size, size), jnp.bfloat16),
-            vmem((size, size), jnp.bfloat16),
-            vmem((size, size), jnp.bfloat16),
-            vmem((size, size), jnp.bfloat16),
-            vmem((size, size), jnp.bfloat16),
-            vmem((size, size), jnp.bfloat16),
+            vmem(flat, jnp.bfloat16),
+            vmem(flat, jnp.bfloat16),
+            square,
+            square,
             vmem((size, size), jnp.float32),
+            square,
+            square,
+            square,
+            square,
+            square,
             vmem((size, width), jnp.bfloat16),
             vmem((size, width), jnp.float32),
-            vmem((size, width), jnp.bfloat16),
+            vmem((shards - 1, rows, width), jnp.bfloat16),
             dma((2,)),
             dma((2, shards - 1)),
             dma((2, shards - 1)),
@@ -365,7 +389,7 @@
         ],
         compiler_params=pltpu.CompilerParams(collective_id=0, has_side_effects=True),
     )(gradient.reshape(flat), momentum.reshape(flat))
-    return (update.reshape(gradient.shape), new_momentum)
+    return (update.reshape(gradient.shape), new_momentum.reshape(gradient.shape))
 
 
 def local(gradient, momentum):
@@ -375,6 +399,7 @@
         lax.axis_size("pair") == 4
         and block_rows * block_cols == 2 * shards
         and rows * shards == size
+        and shards & (shards - 1) == 0
         and rows % 32 == 0
         and size % 256 == 0
     )

time: 38 us -> 36.8 us (0.968)
  other arithmetic: 1.3 us -> 0 us
  local copies, waits for them, and re-layouts: 0.98 us -> 1.94 us
  Pallas kernels: 34.9 us -> 34.1 us
    convert_element_type x1 -> x0, other arithmetic: 1.3 us -> none  [by_kernel(): new_momentum = (decay_rate * momentum.astype(jnp.float32) + gradient.asty...]
    unnamed x7 -> x2, local copies, waits for them, and re-layouts: 0.98 us -> 1.94 us
    pallas_call x1, Pallas kernels: 34.9 us -> 34.1 us  [by_kernel(): pl.pallas_call(functools.partial(step_kernel, shards, block_cols // 2), o...]
where the time goes in v2:
time: 36.8 us; the launch traced here: 36.7 us
  Pallas kernels  34.1 us (93%)
  local copies, waits for them, and re-layouts  1.94 us (5%)
  between operations  0.64 us (2%)
    pallas_call x1, Pallas kernels, by_kernel(): pl.pallas_call(functools.partial(step_kernel, shards, block_cols // 2), o...  34.1 us
    unnamed x2, local copies, waits for them, and re-layouts  1.94 us

profile of v2, /device:TPU:0, one launch (start us, length us, event | category | flops | bytes accessed | tf_op | source)
XLA Modules:
  0.0 36.7 jit_solution(17898854549164310950)
XLA Ops:
  0.6 34.1 %shard_map.41 = (bf16[8,128,512]{2,1,0:T(8,128)(2,1)S(1)}, bf16[8,128,512]{2,1,0:T(8,128)(2,1)S(1)}) custom-call(bf16[8,128,512]{2,1,0:T(8,128)(2,1)} %bitcast.6, bf16[8,128,512]{2,1,0:T(8,128)(2,1)} %bitcast.7), custom_call_target="tpu_custom_call" | custom-call | tf_op jit(solution)/shard_map/pallas_call | solution.py:359
  34.7 1.0 %copy.6 = bf16[1,8,128,512]{3,2,1,0:T(8,128)(2,1)} copy(bf16[1,8,128,512]{3,2,1,0:T(8,128)(2,1)S(1)} %bitcast.5) | data formatting | bytes 2097152
  35.7 1.0 %copy.7 = bf16[1,8,128,512]{3,2,1,0:T(8,128)(2,1)} copy(bf16[1,8,128,512]{3,2,1,0:T(8,128)(2,1)S(1)} %bitcast.4) | data formatting | bytes 2097152

commit v3 on v2

--- a/solution.py
+++ b/solution.py
@@ -115,12 +115,11 @@
     grad_block,
     mom_block,
     full,
-    left_scaled,
-    left_square,
-    right_scaled,
-    right_square,
-    left_factor,
-    right_factor,
+    power1,
+    power2,
+    power3,
+    high,
+    roots,
     product,
     outgoing,
     local_sem,
@@ -134,6 +133,8 @@
     across_recv,
     twin_send,
     twin_recv,
+    root_send,
+    root_recv,
 ):
     count, rows, size = grad.shape
     half = rows // 2
@@ -234,40 +235,55 @@
     inverse = 1.0 / scaling
     identity = diagonal(size, size, 0)
 
-    def prepare(gram, scaled_ref, square_ref):
-        scaled = gram * (inverse / size) + jnp.where(identity, damping * inverse, 0.0)
-        full[...] = scaled
-        narrow = scaled.astype(jnp.bfloat16)
-        scaled_ref[...] = narrow
-        square_ref[...] = (
-            jnp.where(identity, 0.5625, 0.0) - 0.625 * scaled + dot(narrow, narrow) / 16.0
-        ).astype(jnp.bfloat16)
-
-    def newton(first, scaled_ref, square_ref):
-        second = first + dot(square_ref[...], first.astype(jnp.bfloat16))
-        third = second + dot(square_ref[...], second.astype(jnp.bfloat16))
-        return (first + third) * -0.3125 + dot(
-            scaled_ref[...], third.astype(jnp.bfloat16)
-        ) / 16.0
-
-    prepare(dot(values, values, ((0,), (0,))), right_scaled, right_square)
-    right_factor[...] = (
-        newton(full[:, own_cols], right_scaled, right_square)
-        + jnp.where(diagonal(size, width, side * width), 0.5625, 0.0)
+    @pl.when(side == 0)
+    def _():
+        full[...] = dot(values, values, ((1,), (1,)))
+
+    @pl.when(side == 1)
+    def _():
+        full[...] = dot(values, values, ((0,), (0,)))
+
+    shifted = full[...] * (inverse / size) + jnp.where(identity, damping * inverse - 1.0, 0.0)
+    full[...] = shifted
+    power1[...] = shifted.astype(jnp.bfloat16)
+    squared = dot(power1[...], power1[...])
+    power2[...] = squared.astype(jnp.bfloat16)
+    cubed = dot(power2[...], power1[...])
+    power3[...] = cubed.astype(jnp.bfloat16)
+    high[...] = (
+        (35 / 1024) * full[...]
+        + (-19 / 4096) * squared
+        + (1 / 4096) * cubed
+        - jnp.where(identity, 15 / 128, 0.0)
     ).astype(jnp.bfloat16)
-    prepare(dot(values, values, ((1,), (1,))), left_scaled, left_square)
-    left_factor[...] = (
-        newton(full[...], left_scaled, left_square) + jnp.where(identity, 0.5625, 0.0)
-    ).astype(jnp.bfloat16)
+    full[...] = (5 / 32) * squared - 0.25 * full[...]
+    root_copies = []
+    for index in range(2):
+        part = pl.ds(index * width, width)
+        roots[side, part, :] = (full[part, :] + dot(power3[part, :], high[...])).astype(
+            jnp.bfloat16
+        )
+        copy = pltpu.make_async_remote_copy(
+            src_ref=roots.at[side, part],
+            dst_ref=roots.at[side, part],
+            send_sem=root_send.at[index],
+            recv_sem=root_recv.at[index],
+            device_id={"pair": twin},
+            device_id_type=MESH,
+        )
+        copy.start()
+        root_copies.append(copy)
 
     def multiply_rows(new_rows, own_part, owner):
         product[whole_piece(owner), :] = own_part.astype(jnp.float32) + dot(
-            new_rows, right_factor[...]
+            new_rows, roots[1, :, own_cols]
         )
 
     own_block = block_of(column, shard)
+    mom_passes = collect(1, mom_block)
+    for copy in root_copies:
+        copy.wait_recv()
     multiply_rows(new_mom[own_block], new_mom[own_block, :, own_cols], shard)
-    mom_passes = collect(1, mom_block)
     for copy, origin in zip(mom_passes, peers):
         copy.wait_recv()
         new_rows = combine(mom_block[whole_piece(origin), :], grad_block[whole_piece(origin), :])
@@ -283,30 +299,34 @@
         return (
             (
                 product[whole_piece(owner), :]
-                + dot(left_factor[whole_piece(owner), :], narrow_product)
+                + dot(roots[0, whole_piece(owner), :], narrow_product)
             )
             * outer
         ).astype(jnp.bfloat16)
 
+    def part_rows(part):
+        return pl.ds(part * half, half)
+
     backs = []
     for index, target in enumerate(peers):
         outgoing[index] = update_rows(target)
+        for part in range(2):
+            copy = pltpu.make_async_remote_copy(
+                src_ref=outgoing.at[index, part_rows(part)],
+                dst_ref=update.at[own_block, part_rows(part), own_cols],
+                send_sem=back_send.at[2 * index + part],
+                recv_sem=back_recv.at[2 * index + part],
+                device_id={"shard": target},
+                device_id_type=MESH,
+            )
+            copy.start()
+            backs.append(copy)
+    update[own_block, :, own_cols] = update_rows(shard)
+
+    def hand_on(block, part, send, recv, index, peer):
         copy = pltpu.make_async_remote_copy(
-            src_ref=outgoing.at[index],
-            dst_ref=update.at[own_block, :, own_cols],
-            send_sem=back_send.at[index],
-            recv_sem=back_recv.at[index],
-            device_id={"shard": target},
-            device_id_type=MESH,
-        )
-        copy.start()
-        backs.append(copy)
-    update[own_block, :, own_cols] = update_rows(shard)
-
-    def hand_on(block, send, recv, index, peer):
-        copy = pltpu.make_async_remote_copy(
-            src_ref=update.at[block, :, own_cols],
-            dst_ref=update.at[block, :, own_cols],
+            src_ref=update.at[block, part_rows(part), own_cols],
+            dst_ref=update.at[block, part_rows(part), own_cols],
             send_sem=send.at[index],
             recv_sem=recv.at[index],
             device_id={"pair": peer},
@@ -315,31 +335,55 @@
         copy.start()
         return copy
 
+    origins = [shard] + peers
     acrosses = []
     twins = []
 
-    def take_across(index, origin):
+    def take_across(index):
         acrosses[index].wait_recv()
+        block = block_of(1 - column, origins[index // 2])
         twins.append(
-            hand_on(block_of(1 - column, origin), twin_send, twin_recv, shards + index, twin)
-        )
-
-    origins = [shard] + peers
-    for index, origin in enumerate(origins):
-        if index:
-            backs[index - 1].wait_recv()
-        block = block_of(column, origin)
-        acrosses.append(hand_on(block, across_send, across_recv, index, across))
-        twins.append(hand_on(block, twin_send, twin_recv, index, twin))
-        if index:
-            take_across(index - 1, origins[index - 1])
-    take_across(shards - 1, origins[-1])
+            hand_on(block, index % 2, twin_send, twin_recv, 2 * shards + index, twin)
+        )
+
+    for index in range(2 * shards):
+        if index >= 2:
+            backs[index - 2].wait_recv()
+        block = block_of(column, origins[index // 2])
+        acrosses.append(hand_on(block, index % 2, across_send, across_recv, index, across))
+        twins.append(hand_on(block, index % 2, twin_send, twin_recv, index, twin))
+        if index >= 2:
+            take_across(index - 2)
+    take_across(2 * shards - 2)
+    take_across(2 * shards - 1)
     for copy in twins:
         copy.wait_recv()
     for copy in (
-        sends[0] + sends[1] + grad_passes + mom_passes + backs + acrosses + twins
+        sends[0]
+        + sends[1]
+        + grad_passes
+        + mom_passes
+        + root_copies
+        + backs
+        + acrosses
+        + twins
     ):
         copy.wait_send()
+
+
+def store_kernel(parts, update, new_mom, update_out, new_mom_out, sems):
+    size = update.shape[0] // parts
+    copies = []
+    for kind, (source, target) in enumerate(((update, update_out), (new_mom, new_mom_out))):
+        for part in range(parts):
+            piece = pl.ds(part * size, size)
+            copy = pltpu.make_async_copy(
+                source.at[piece], target.at[piece], sems.at[kind, part]
+            )
+            copy.start()
+            copies.append(copy)
+    for copy in copies:
+        copy.wait()
 
 
 def peer_order(shards):
@@ -371,8 +415,7 @@
             square,
             square,
             square,
-            square,
-            vmem((size, width), jnp.bfloat16),
+            vmem((2, size, size), jnp.bfloat16),
             vmem((size, width), jnp.float32),
             vmem((shards - 1, rows, width), jnp.bfloat16),
             dma((2,)),
@@ -380,15 +423,24 @@
             dma((2, shards - 1)),
             dma((2, shards - 1)),
             dma((2, shards - 1)),
-            dma((shards - 1,)),
-            dma((shards - 1,)),
-            dma((shards,)),
-            dma((shards,)),
+            dma((2 * shards - 2,)),
+            dma((2 * shards - 2,)),
             dma((2 * shards,)),
             dma((2 * shards,)),
+            dma((4 * shards,)),
+            dma((4 * shards,)),
+            dma((2,)),
+            dma((2,)),
         ],
         compiler_params=pltpu.CompilerParams(collective_id=0, has_side_effects=True),
     )(gradient.reshape(flat), momentum.reshape(flat))
+    update, new_momentum = pl.pallas_call(
+        functools.partial(store_kernel, 4),
+        out_shape=[jax.ShapeDtypeStruct(flat, jnp.bfloat16)] * 2,
+        in_specs=[pl.BlockSpec(memory_space=pl.ANY)] * 2,
+        out_specs=[pl.BlockSpec(memory_space=pl.ANY)] * 2,
+        scratch_shapes=[dma((2, 4))],
+    )(update, new_momentum)
     return (update.reshape(gradient.shape), new_momentum.reshape(gradient.shape))
 
 

time: 36.8 us -> 102 us (2.77)
  Pallas kernels: 34.1 us -> 99.6 us
    pallas_call x0 -> x1, Pallas kernels: none -> 64.7 us  [by_kernel(): pl.pallas_call(functools.partial(store_kernel, 4), out_shape=[jax.ShapeDt...]
where the time goes in v3:
time: 102 us
  Pallas kernels  99.6 us (98%)
  local copies, waits for them, and re-layouts  1.97 us (2%)
    pallas_call x1, Pallas kernels, by_kernel(): pl.pallas_call(functools.partial(store_kernel, 4), out_shape=[jax.ShapeDt...  64.7 us
    pallas_call x1, Pallas kernels, by_kernel(): pl.pallas_call(functools.partial(step_kernel, shards, block_cols // 2), o...  34.9 us

profile of v3, /device:TPU:0, one launch (start us, length us, event | category | flops | bytes accessed | tf_op | source)
XLA Modules:
  0.0 102.2 jit_solution(11995726747885062545)
XLA Ops:
  0.6 34.9 %shard_map.41 = (bf16[8,128,512]{2,1,0:T(8,128)(2,1)S(1)}, bf16[8,128,512]{2,1,0:T(8,128)(2,1)S(1)}) custom-call(bf16[8,128,512]{2,1,0:T(8,128)(2,1)} %bitcast.4, bf16[8,128,512]{2,1,0:T(8,128)(2,1)} %bitcast.5), custom_call_target="tpu_custom_call" | custom-call | tf_op jit(solution)/shard_map/pallas_call | solution.py:403
  35.5 0.0 copy-start
  35.5 1.0 copy-done
  36.5 0.0 copy-start.1
  36.5 1.0 copy-done.1
  37.5 64.7 %shard_map.42 = (bf16[8,128,512]{2,1,0:T(8,128)(2,1)}, bf16[8,128,512]{2,1,0:T(8,128)(2,1)}) custom-call(bf16[8,128,512]{2,1,0:T(8,128)(2,1)} %copy-done, bf16[8,128,512]{2,1,0:T(8,128)(2,1)} %copy-done.1), custom_call_target="tpu_custom_call" | custom-call | tf_op jit(solution)/shard_map/pallas_call | solution.py:437
Async XLA Ops:
  35.5 1.0 copy-start
  36.5 1.0 copy-start.1

commit v4 on v3

--- a/solution.py
+++ b/solution.py
@@ -371,21 +371,6 @@
         copy.wait_send()
 
 
-def store_kernel(parts, update, new_mom, update_out, new_mom_out, sems):
-    size = update.shape[0] // parts
-    copies = []
-    for kind, (source, target) in enumerate(((update, update_out), (new_mom, new_mom_out))):
-        for part in range(parts):
-            piece = pl.ds(part * size, size)
-            copy = pltpu.make_async_copy(
-                source.at[piece], target.at[piece], sems.at[kind, part]
-            )
-            copy.start()
-            copies.append(copy)
-    for copy in copies:
-        copy.wait()
-
-
 def peer_order(shards):
     masks = list(range(1, shards))
     return masks[:1] + masks[:0:-1]
@@ -434,13 +419,6 @@
         ],
         compiler_params=pltpu.CompilerParams(collective_id=0, has_side_effects=True),
     )(gradient.reshape(flat), momentum.reshape(flat))
-    update, new_momentum = pl.pallas_call(
-        functools.partial(store_kernel, 4),
-        out_shape=[jax.ShapeDtypeStruct(flat, jnp.bfloat16)] * 2,
-        in_specs=[pl.BlockSpec(memory_space=pl.ANY)] * 2,
-        out_specs=[pl.BlockSpec(memory_space=pl.ANY)] * 2,
-        scratch_shapes=[dma((2, 4))],
-    )(update, new_momentum)
     return (update.reshape(gradient.shape), new_momentum.reshape(gradient.shape))
 
 

time: 102 us -> 37.6 us (0.37)
  Pallas kernels: 99.6 us -> 34.9 us
    pallas_call x1 -> x0, Pallas kernels: 64.7 us -> none  [by_kernel(): pl.pallas_call(functools.partial(store_kernel, 4), out_shape=[jax.ShapeDt...]
where the time goes in v4:
time: 37.6 us; the launch traced here: 37.5 us
  Pallas kernels  34.9 us (93%)
  local copies, waits for them, and re-layouts  1.94 us (5%)
  between operations  0.64 us (2%)
    pallas_call x1, Pallas kernels, by_kernel(): pl.pallas_call(functools.partial(step_kernel, shards, block_cols // 2), o...  34.9 us
    unnamed x2, local copies, waits for them, and re-layouts  1.94 us

profile of v4, /device:TPU:0, one launch (start us, length us, event | category | flops | bytes accessed | tf_op | source)
XLA Modules:
  0.0 37.5 jit_solution(683331374722393731)
XLA Ops:
  0.6 34.9 %shard_map.41 = (bf16[8,128,512]{2,1,0:T(8,128)(2,1)S(1)}, bf16[8,128,512]{2,1,0:T(8,128)(2,1)S(1)}) custom-call(bf16[8,128,512]{2,1,0:T(8,128)(2,1)} %bitcast.6, bf16[8,128,512]{2,1,0:T(8,128)(2,1)} %bitcast.7), custom_call_target="tpu_custom_call" | custom-call | tf_op jit(solution)/shard_map/pallas_call | solution.py:388
  35.5 1.0 %copy.6 = bf16[1,8,128,512]{3,2,1,0:T(8,128)(2,1)} copy(bf16[1,8,128,512]{3,2,1,0:T(8,128)(2,1)S(1)} %bitcast.5) | data formatting | bytes 2097152
  36.5 1.0 %copy.7 = bf16[1,8,128,512]{3,2,1,0:T(8,128)(2,1)} copy(bf16[1,8,128,512]{3,2,1,0:T(8,128)(2,1)S(1)} %bitcast.4) | data formatting | bytes 2097152

commit v5 on v4

--- a/solution.py
+++ b/solution.py
@@ -135,6 +135,7 @@
     twin_recv,
     root_send,
     root_recv,
+    seen,
 ):
     count, rows, size = grad.shape
     half = rows // 2
@@ -145,16 +146,13 @@
     column = pair // 2
     twin = pair + 1 - 2 * side
     across = lax.rem(pair + 2, 4)
-    order = peer_order(shards)
+    last = shards - 1
+    lower = 1 - shard // (shards // 2)
+    place = lower * shard + (1 - lower) * (last - shard)
     peers = []
-    for mask in order:
-        peer = shard
-        bit = 1
-        while bit < shards:
-            if mask & bit:
-                peer = peer + bit - 2 * bit * lax.rem(shard // bit, 2)
-            bit *= 2
-        peers.append(peer)
+    for step in range(last):
+        mirrored = step + (step - place + shards) // shards
+        peers.append(lower * mirrored + (1 - lower) * (last - mirrored))
 
     def block_of(column_half, owner):
         return (owner // half_cols) * 2 * half_cols + column_half * half_cols + lax.rem(
@@ -162,8 +160,18 @@
         )
 
     barrier = pltpu.get_barrier_semaphore()
-    for peer in peers:
-        pl.semaphore_signal(barrier, inc=1, device_id={"shard": peer}, device_id_type=MESH)
+
+    def greet(semaphore, peer):
+        pl.semaphore_signal(semaphore, inc=1, device_id={"shard": peer}, device_id_type=MESH)
+
+    @pl.when(shard > 0)
+    def _():
+        greet(barrier, shard - 1)
+
+    @pl.when(shard < last)
+    def _():
+        greet(barrier, shard + 1)
+
     for peer in (twin, across):
         pl.semaphore_signal(barrier, inc=1, device_id={"pair": peer}, device_id_type=MESH)
     loads = []
@@ -171,7 +179,7 @@
         copy = pltpu.make_async_copy(source, local_rows, local_sem.at[kind])
         copy.start()
         loads.append(copy)
-    pl.semaphore_wait(barrier, shards + 1)
+    pl.semaphore_wait(barrier, 2 + (shard + last) // shards + (2 * last - shard) // shards)
 
     def piece(owner):
         return pl.ds(pl.multiple_of(owner * rows + side * half, half), half)
@@ -181,21 +189,49 @@
 
     own_half = pl.ds(pl.multiple_of(side * half, half), half)
     own_cols = pl.ds(pl.multiple_of(side * width, width), width)
-    sends = []
-    for kind, (source, block) in enumerate(((grad, grad_block), (mom, mom_block))):
-        kind_sends = []
-        for index, target in enumerate(peers):
-            copy = pltpu.make_async_remote_copy(
-                src_ref=source.at[block_of(column, target), own_half],
-                dst_ref=block.at[piece(shard)],
-                send_sem=z_send.at[kind, index],
-                recv_sem=z_recv.at[kind, index],
-                device_id={"shard": target},
-                device_id_type=MESH,
-            )
-            copy.start()
-            kind_sends.append(copy)
-        sends.append(kind_sends)
+    def row_copy(kind, target, origin):
+        source, block = ((grad, grad_block), (mom, mom_block))[kind]
+        return pltpu.make_async_remote_copy(
+            src_ref=source.at[block_of(column, target), own_half],
+            dst_ref=block.at[piece(origin)],
+            send_sem=z_send.at[kind, target],
+            recv_sem=z_recv.at[kind, origin],
+            device_id={"shard": target},
+            device_id_type=MESH,
+        )
+
+    for distance in range(1, shards):
+        if distance > 1:
+
+            @pl.when(shard >= distance - 1)
+            def _():
+                @pl.when(shard < last)
+                def _():
+                    greet(seen.at[0, distance - 2], shard + 1)
+
+            @pl.when(shard <= last - (distance - 1))
+            def _():
+                @pl.when(shard > 0)
+                def _():
+                    greet(seen.at[1, distance - 2], shard - 1)
+
+        @pl.when(shard <= last - distance)
+        def _():
+            if distance > 1:
+                pl.semaphore_wait(seen.at[1, distance - 2], 1)
+            row_copy(0, shard + distance, shard).start()
+
+        @pl.when(shard >= distance)
+        def _():
+            if distance > 1:
+                pl.semaphore_wait(seen.at[0, distance - 2], 1)
+            row_copy(0, shard - distance, shard).start()
+
+    sends = [row_copy(0, target, shard) for target in peers]
+    for target in peers:
+        copy = row_copy(1, target, shard)
+        copy.start()
+        sends.append(copy)
 
     def combine(momentum, gradient):
         return (
@@ -211,7 +247,7 @@
     def collect(kind, block):
         passes = []
         for index, origin in enumerate(peers):
-            sends[kind][index].wait_recv()
+            row_copy(kind, shard, origin).wait_recv()
             copy = pltpu.make_async_remote_copy(
                 src_ref=block.at[piece(origin)],
                 dst_ref=block.at[piece(origin)],
@@ -304,29 +340,28 @@
             * outer
         ).astype(jnp.bfloat16)
 
-    def part_rows(part):
-        return pl.ds(part * half, half)
+    def back_copy(index, target, origin):
+        return pltpu.make_async_remote_copy(
+            src_ref=outgoing.at[index],
+            dst_ref=update.at[block_of(column, origin), :, own_cols],
+            send_sem=back_send.at[index],
+            recv_sem=back_recv.at[origin],
+            device_id={"shard": target},
+            device_id_type=MESH,
+        )
 
     backs = []
     for index, target in enumerate(peers):
         outgoing[index] = update_rows(target)
-        for part in range(2):
-            copy = pltpu.make_async_remote_copy(
-                src_ref=outgoing.at[index, part_rows(part)],
-                dst_ref=update.at[own_block, part_rows(part), own_cols],
-                send_sem=back_send.at[2 * index + part],
-                recv_sem=back_recv.at[2 * index + part],
-                device_id={"shard": target},
-                device_id_type=MESH,
-            )
-            copy.start()
-            backs.append(copy)
+        copy = back_copy(index, target, shard)
+        copy.start()
+        backs.append(copy)
     update[own_block, :, own_cols] = update_rows(shard)
 
-    def hand_on(block, part, send, recv, index, peer):
+    def hand_on(block, send, recv, index, peer):
         copy = pltpu.make_async_remote_copy(
-            src_ref=update.at[block, part_rows(part), own_cols],
-            dst_ref=update.at[block, part_rows(part), own_cols],
+            src_ref=update.at[block, :, own_cols],
+            dst_ref=update.at[block, :, own_cols],
             send_sem=send.at[index],
             recv_sem=recv.at[index],
             device_id={"pair": peer},
@@ -341,26 +376,22 @@
 
     def take_across(index):
         acrosses[index].wait_recv()
-        block = block_of(1 - column, origins[index // 2])
-        twins.append(
-            hand_on(block, index % 2, twin_send, twin_recv, 2 * shards + index, twin)
-        )
-
-    for index in range(2 * shards):
-        if index >= 2:
-            backs[index - 2].wait_recv()
-        block = block_of(column, origins[index // 2])
-        acrosses.append(hand_on(block, index % 2, across_send, across_recv, index, across))
-        twins.append(hand_on(block, index % 2, twin_send, twin_recv, index, twin))
-        if index >= 2:
-            take_across(index - 2)
-    take_across(2 * shards - 2)
-    take_across(2 * shards - 1)
+        block = block_of(1 - column, origins[index])
+        twins.append(hand_on(block, twin_send, twin_recv, shards + index, twin))
+
+    for index, origin in enumerate(origins):
+        if index:
+            back_copy(index - 1, shard, origin).wait_recv()
+        block = block_of(column, origin)
+        acrosses.append(hand_on(block, across_send, across_recv, index, across))
+        twins.append(hand_on(block, twin_send, twin_recv, index, twin))
+        if index:
+            take_across(index - 1)
+    take_across(last)
     for copy in twins:
         copy.wait_recv()
     for copy in (
-        sends[0]
-        + sends[1]
+        sends
         + grad_passes
         + mom_passes
         + root_copies
@@ -369,11 +400,6 @@
         + twins
     ):
         copy.wait_send()
-
-
-def peer_order(shards):
-    masks = list(range(1, shards))
-    return masks[:1] + masks[:0:-1]
 
 
 def by_kernel(gradient, momentum):
@@ -404,18 +430,19 @@
             vmem((size, width), jnp.float32),
             vmem((shards - 1, rows, width), jnp.bfloat16),
             dma((2,)),
+            dma((2, shards)),
+            dma((2, shards)),
             dma((2, shards - 1)),
             dma((2, shards - 1)),
-            dma((2, shards - 1)),
-            dma((2, shards - 1)),
-            dma((2 * shards - 2,)),
-            dma((2 * shards - 2,)),
+            dma((shards - 1,)),
+            dma((shards,)),
+            dma((shards,)),
+            dma((shards,)),
             dma((2 * shards,)),
             dma((2 * shards,)),
-            dma((4 * shards,)),
-            dma((4 * shards,)),
             dma((2,)),
             dma((2,)),
+            pltpu.SemaphoreType.REGULAR((2, max(shards - 2, 1))),
         ],
         compiler_params=pltpu.CompilerParams(collective_id=0, has_side_effects=True),
     )(gradient.reshape(flat), momentum.reshape(flat))
@@ -429,7 +456,7 @@
         lax.axis_size("pair") == 4
         and block_rows * block_cols == 2 * shards
         and rows * shards == size
-        and shards & (shards - 1) == 0
+        and shards % 2 == 0
         and rows % 32 == 0
         and size % 256 == 0
     )

time: 37.6 us -> 35.4 us (0.941)
  Pallas kernels: 34.9 us -> 32.4 us
    pallas_call x1, Pallas kernels: 34.9 us -> 32.4 us  [by_kernel(): pl.pallas_call(functools.partial(step_kernel, shards, block_cols // 2), o...]
where the time goes in v5:
time: 35.4 us; the launch traced here: 35 us
  Pallas kernels  32.4 us (92%)
  local copies, waits for them, and re-layouts  1.94 us (5%)
  between operations  0.64 us (2%)
    pallas_call x1, Pallas kernels, by_kernel(): pl.pallas_call(functools.partial(step_kernel, shards, block_cols // 2), o...  32.4 us
    unnamed x2, local copies, waits for them, and re-layouts  1.94 us

profile of v5, /device:TPU:0, one launch (start us, length us, event | category | flops | bytes accessed | tf_op | source)
XLA Modules:
  0.0 35.0 jit_solution(11047691101952021491)
XLA Ops:
  0.6 32.4 %shard_map.41 = (bf16[8,128,512]{2,1,0:T(8,128)(2,1)S(1)}, bf16[8,128,512]{2,1,0:T(8,128)(2,1)S(1)}) custom-call(bf16[8,128,512]{2,1,0:T(8,128)(2,1)} %bitcast.6, bf16[8,128,512]{2,1,0:T(8,128)(2,1)} %bitcast.7), custom_call_target="tpu_custom_call" | custom-call | tf_op jit(solution)/shard_map/pallas_call | solution.py:414
  33.0 1.0 %copy.6 = bf16[1,8,128,512]{3,2,1,0:T(8,128)(2,1)} copy(bf16[1,8,128,512]{3,2,1,0:T(8,128)(2,1)S(1)} %bitcast.5) | data formatting | bytes 2097152
  34.0 1.0 %copy.7 = bf16[1,8,128,512]{3,2,1,0:T(8,128)(2,1)} copy(bf16[1,8,128,512]{3,2,1,0:T(8,128)(2,1)S(1)} %bitcast.4) | data formatting | bytes 2097152

commit v6 on v5

--- a/solution.py
+++ b/solution.py
@@ -350,14 +350,6 @@
             device_id_type=MESH,
         )
 
-    backs = []
-    for index, target in enumerate(peers):
-        outgoing[index] = update_rows(target)
-        copy = back_copy(index, target, shard)
-        copy.start()
-        backs.append(copy)
-    update[own_block, :, own_cols] = update_rows(shard)
-
     def hand_on(block, send, recv, index, peer):
         copy = pltpu.make_async_remote_copy(
             src_ref=update.at[block, :, own_cols],
@@ -370,23 +362,34 @@
         copy.start()
         return copy
 
-    origins = [shard] + peers
     acrosses = []
     twins = []
+
+    def spread(block, index):
+        acrosses.append(hand_on(block, across_send, across_recv, index, across))
+        twins.append(hand_on(block, twin_send, twin_recv, index, twin))
+
+    backs = []
+    for index, target in enumerate(peers):
+        outgoing[index] = update_rows(target)
+        copy = back_copy(index, target, shard)
+        copy.start()
+        backs.append(copy)
+        if index == 0:
+            update[own_block, :, own_cols] = update_rows(shard)
+            spread(own_block, 0)
+
+    origins = [shard] + peers
 
     def take_across(index):
         acrosses[index].wait_recv()
         block = block_of(1 - column, origins[index])
         twins.append(hand_on(block, twin_send, twin_recv, shards + index, twin))
 
-    for index, origin in enumerate(origins):
-        if index:
-            back_copy(index - 1, shard, origin).wait_recv()
-        block = block_of(column, origin)
-        acrosses.append(hand_on(block, across_send, across_recv, index, across))
-        twins.append(hand_on(block, twin_send, twin_recv, index, twin))
-        if index:
-            take_across(index - 1)
+    for index in range(1, shards):
+        back_copy(index - 1, shard, origins[index]).wait_recv()
+        spread(block_of(column, origins[index]), index)
+        take_across(index - 1)
     take_across(last)
     for copy in twins:
         copy.wait_recv()

time: 35.4 us -> 35.4 us (level)
  no operation moved by 1% of the time
where the time goes in v6:
time: 35.4 us; the launch traced here: 35 us
  Pallas kernels  32.4 us (92%)
  local copies, waits for them, and re-layouts  1.94 us (5%)
  between operations  0.64 us (2%)
    pallas_call x1, Pallas kernels, by_kernel(): pl.pallas_call(functools.partial(step_kernel, shards, block_cols // 2), o...  32.4 us
    unnamed x2, local copies, waits for them, and re-layouts  1.94 us

profile of v6, /device:TPU:0, one launch (start us, length us, event | category | flops | bytes accessed | tf_op | source)
XLA Modules:
  0.0 35.0 jit_solution(17524523080084656444)
XLA Ops:
  0.6 32.4 %shard_map.41 = (bf16[8,128,512]{2,1,0:T(8,128)(2,1)S(1)}, bf16[8,128,512]{2,1,0:T(8,128)(2,1)S(1)}) custom-call(bf16[8,128,512]{2,1,0:T(8,128)(2,1)} %bitcast.6, bf16[8,128,512]{2,1,0:T(8,128)(2,1)} %bitcast.7), custom_call_target="tpu_custom_call" | custom-call | tf_op jit(solution)/shard_map/pallas_call | solution.py:417
  33.0 1.0 %copy.6 = bf16[1,8,128,512]{3,2,1,0:T(8,128)(2,1)} copy(bf16[1,8,128,512]{3,2,1,0:T(8,128)(2,1)S(1)} %bitcast.5) | data formatting | bytes 2097152
  34.0 1.0 %copy.7 = bf16[1,8,128,512]{3,2,1,0:T(8,128)(2,1)} copy(bf16[1,8,128,512]{3,2,1,0:T(8,128)(2,1)S(1)} %bitcast.4) | data formatting | bytes 2097152
